TPU v7x, 256 devices: a whole 4x4x8 slice. The times are simulated.
256 devices in a mesh: row: 64 (over z, y, core), col: 4 (over x).
Axes of the slice: x: 4, y: 4, z: 8, core: 2. Of those that a mesh axis runs over, the one named last changes fastest.
Arguments:
- train_points: float32 [16, 3, 64, 128], P(None, None, 'row'), may hold values from -6 to 6
- new_points: float32 [16, 256], replicated, may hold values from -6 to 6
- lengthscales: float32 [16], replicated, may hold values from 2.5 to 6
- factor: float32 [3, 64, 128, 3, 4, 2048], P(None, 'row', None, None, 'col'), may hold values from -0.02734375 to 0.02734375
- diag_inverse: float32 [3, 64, 128, 4, 2048], P(None, 'row', None, 'col'), may hold values from -3 to 3
Outputs:
- solution: float32 [3, 4, 64, 32, 256], P(None, 'col', 'row')
All inputs are finite; a program needn't handle non-finite values.
Results may differ from a plain program's by a relative error of at most 0.0001.
Values sent between devices are 32-bit elements; how exact they have to be, the bound alone decides.
No kernel may reach another device: no remote copies, remote signals or barrier semaphores. Data moves between devices by JAX's collectives and lax.ppermute only.
A program may use at most 128 MiB of HBM per device.

v0:
```python
import jax
import jax.numpy as jnp
from jax import lax
from jax.sharding import PartitionSpec as P


def on_device(train_points, new_points, lengthscales, factor, diag_inverse):
    highest = lax.Precision.HIGHEST
    panels = factor.shape[0]
    block_rows = factor.shape[2]
    quarter_cols = factor.shape[5]
    new_count = new_points.shape[1]
    share_rows = block_rows // lax.axis_size("col")
    scaled_train = (train_points / lengthscales[:, None, None, None]).reshape(
        train_points.shape[0], panels * block_rows
    )
    scaled_new = new_points / lengthscales[:, None]
    inner_products = jnp.dot(scaled_train.T, scaled_new, precision=highest)
    sqdist = (
        jnp.sum(scaled_train * scaled_train, axis=0)[:, None]
        + jnp.sum(scaled_new * scaled_new, axis=0)[None, :]
        - 2.0 * inner_products
    )
    kernel = jnp.exp(-0.5 * sqdist).reshape(panels, block_rows, new_count)
    factor_blocks = factor.reshape(panels, block_rows, panels, quarter_cols)
    inverse_blocks = diag_inverse.reshape(panels, block_rows, quarter_cols)
    panel_numbers = jnp.arange(panels)

    def update(partial_rows, panel, quarter, after):
        column_slab = lax.dynamic_index_in_dim(factor_blocks, panel, axis=2, keepdims=False)
        change = jnp.einsum("piq,qm->pim", column_slab, quarter, precision=highest)
        below = (panel_numbers > after)[:, None, None]
        return partial_rows + jnp.where(below, change, 0.0)

    def advance(panel, loop_state):
        partial_rows, solved, pending = loop_state
        own_partial = lax.dynamic_index_in_dim(partial_rows, panel, 0, keepdims=False)
        summed = lax.psum(own_partial, "col")
        residual = lax.dynamic_index_in_dim(kernel, panel, 0, keepdims=False) - summed
        inverse_block = lax.dynamic_index_in_dim(inverse_blocks, panel, 0, keepdims=False)
        product = jnp.einsum("iq,im->qm", inverse_block, residual, precision=highest)
        own_rows = lax.psum_scatter(product, "row", scatter_dimension=0, tiled=True)
        quarter = lax.all_gather(own_rows, "row", axis=0, tiled=True)
        solved = lax.dynamic_update_index_in_dim(solved, own_rows, panel, 0)
        partial_rows = update(partial_rows, panel, quarter, panel)
        return (partial_rows, solved, pending)

    initial = (
        jnp.zeros((panels, block_rows, new_count), jnp.float32),
        jnp.zeros((panels, share_rows, new_count), jnp.float32),
        jnp.zeros((quarter_cols, new_count), jnp.float32),
    )
    partial_rows, solved, pending = lax.fori_loop(0, panels, advance, initial)
    return solved.reshape(panels, 1, 1, share_rows, new_count)


def solution(mesh):
    return jax.shard_map(
        on_device,
        mesh=mesh,
        in_specs=(
            P(None, None, "row", None),
            P(),
            P(),
            P(None, "row", None, None, "col", None),
            P(None, "row", None, "col", None),
        ),
        out_specs=P(None, "col", "row", None, None),
        check_vma=False,
    )
```

profile of v0, /device:TPU:1, one launch (start us, length us, event | category | flops | bytes accessed | tf_op | source)
XLA Modules:
  0.0 868.2 jit_solution(1024487664733539460)
XLA Ops:
  6.5 0.9 fusion.27
  7.4 0.8 multiply_reduce_fusion.1
  8.3 2.0 fusion.24
  10.3 12.1 %copy.15 = f32[3,1,128,3,1,2048]{5,2,0,3,4,1:T(8,128)} copy(f32[3,1,128,3,1,2048]{5,4,3,2,1,0:T(1,128)} %param.10) | data formatting | bytes 18874368 | tf_op args[3]
  22.4 0.0 copy-done
  22.4 1.4 copy.16
  23.8 837.8 %while.16 = (s32[]{:T(128)}, f32[3,128,256]{2,1,0:T(8,128)}, f32[3,32,256]{2,1,0:T(8,128)}, f32[3,128,3,2048]{3,1,0,2:T(8,128)}, f32[3,128,2048]{2,1,0:T(8,128)S...) while((s32[]{:T(128)}, f32[3,128,256]{2,1,0:T(8,128)}, f32[3,32,256]{2,1,0:T(8,128)}, ...), condition=%wide.region_5.6_spmd.clone, body=%wide.region_2.5_spmd.clone.sunk | while | flops 3221585920 | bytes 24118516 | solution.py:53
  24.0 0.0 all-reduce.2.cloned.1.call-start
  24.1 0.7 dynamic-slice_bitcast_fusion.2
  24.8 0.0 all-reduce.2.cloned.1.call-update
  24.8 0.0 reduce-scatter.2.cloned.1.call-start
  24.9 50.3 %all-reduce.2.cloned.1.call-done = f32[128,256]{1,0:T(8,128)} async-done(((f32[128,256]{1,0:T(8,128)}), f32[128,256]{1,0:T(8,128)}) %all-reduce.2.cloned.1.call-update) | async-done | bytes 131088 | tf_op jit(solution)/shard_map/while/body/eval_jaxpr/psum | solution.py:38
  75.2 4.1 fusion.36
  79.3 0.0 reduce-scatter.2.cloned.1.call-update
  79.3 0.0 all-gather.2.cloned.1.call-start
  79.4 138.6 %reduce-scatter.2.cloned.1.call-done = f32[32,256]{1,0:T(8,128)} async-done(((f32[2048,256]{1,0:T(8,128)}), f32[32,256]{1,0:T(8,128)}) %reduce-scatter.2.cloned.1.call-update) | async-done | bytes 32784 | tf_op jit(solution)/shard_map/while/body/eval_jaxpr/reduce_scatter | solution.py:42
  218.0 0.0 all-gather.2.cloned.1.call-update
  218.1 1.4 bitcast_dynamic-update-slice_fusion.2
  219.4 82.4 %all-gather.2.cloned.1.call-done = f32[2048,256]{1,0:T(8,128)} async-done(((f32[32,256]{1,0:T(8,128)}), f32[2048,256]{1,0:T(8,128)}) %all-gather.2.cloned.1.call-update) | async-done | bytes 2097168 | tf_op jit(solution)/shard_map/while/body/eval_jaxpr/all_gather | solution.py:43
  301.9 6.0 fusion.37
  307.8 0.0 all-reduce.2.cloned.1.call-start
  307.8 1.0 broadcast_select_fusion.2
  308.9 0.7 dynamic-slice_bitcast_fusion.2
  309.5 0.0 all-reduce.2.cloned.1.call-update
  309.6 0.0 reduce-scatter.2.cloned.1.call-start
  309.6 42.5 %all-reduce.2.cloned.1.call-done = f32[128,256]{1,0:T(8,128)} async-done(((f32[128,256]{1,0:T(8,128)}), f32[128,256]{1,0:T(8,128)}) %all-reduce.2.cloned.1.call-update) | async-done | bytes 131088 | tf_op jit(solution)/shard_map/while/body/eval_jaxpr/psum | solution.py:38
  352.1 4.1 fusion.36
  356.2 0.0 reduce-scatter.2.cloned.1.call-update
  356.2 0.0 all-gather.2.cloned.1.call-start
  356.3 138.2 %reduce-scatter.2.cloned.1.call-done = f32[32,256]{1,0:T(8,128)} async-done(((f32[2048,256]{1,0:T(8,128)}), f32[32,256]{1,0:T(8,128)}) %reduce-scatter.2.cloned.1.call-update) | async-done | bytes 32784 | tf_op jit(solution)/shard_map/while/body/eval_jaxpr/reduce_scatter | solution.py:42
  494.5 0.0 all-gather.2.cloned.1.call-update
  494.5 1.4 bitcast_dynamic-update-slice_fusion.2
  495.9 82.6 %all-gather.2.cloned.1.call-done = f32[2048,256]{1,0:T(8,128)} async-done(((f32[32,256]{1,0:T(8,128)}), f32[2048,256]{1,0:T(8,128)}) %all-gather.2.cloned.1.call-update) | async-done | bytes 2097168 | tf_op jit(solution)/shard_map/while/body/eval_jaxpr/all_gather | solution.py:43
  578.5 6.0 fusion.37
  584.4 0.0 all-reduce.2.cloned.1.call-start
  584.5 1.0 broadcast_select_fusion.2
  585.5 0.7 dynamic-slice_bitcast_fusion.2
  586.1 0.0 all-reduce.2.cloned.1.call-update
  586.2 0.0 reduce-scatter.2.cloned.1.call-start
  586.2 42.8 %all-reduce.2.cloned.1.call-done = f32[128,256]{1,0:T(8,128)} async-done(((f32[128,256]{1,0:T(8,128)}), f32[128,256]{1,0:T(8,128)}) %all-reduce.2.cloned.1.call-update) | async-done | bytes 131088 | tf_op jit(solution)/shard_map/while/body/eval_jaxpr/psum | solution.py:38
  629.0 4.1 fusion.36
  633.2 0.0 reduce-scatter.2.cloned.1.call-update
  633.2 0.0 all-gather.2.cloned.1.call-start
  633.2 138.6 %reduce-scatter.2.cloned.1.call-done = f32[32,256]{1,0:T(8,128)} async-done(((f32[2048,256]{1,0:T(8,128)}), f32[32,256]{1,0:T(8,128)}) %reduce-scatter.2.cloned.1.call-update) | async-done | bytes 32784 | tf_op jit(solution)/shard_map/while/body/eval_jaxpr/reduce_scatter | solution.py:42
  771.9 0.0 all-gather.2.cloned.1.call-update
  771.9 1.4 bitcast_dynamic-update-slice_fusion.2
  773.3 82.4 %all-gather.2.cloned.1.call-done = f32[2048,256]{1,0:T(8,128)} async-done(((f32[32,256]{1,0:T(8,128)}), f32[2048,256]{1,0:T(8,128)}) %all-gather.2.cloned.1.call-update) | async-done | bytes 2097168 | tf_op jit(solution)/shard_map/while/body/eval_jaxpr/all_gather | solution.py:43
  855.7 6.0 fusion.37
  (7 shorter events, 0.1 us)
Async XLA Ops:
  10.3 12.1 %copy-start = (f32[3,1,128,1,2048]{4,3,2,1,0:T(1,128)S(1)}, f32[3,1,128,1,2048]{4,3,2,1,0:T(1,128)}, u32[]{:S(2)}) copy-start(f32[3,1,128,1,2048]{4,3,2,1,0:T(1,128)} %param.11) | copy-start | bytes 9437188
  24.0 51.2 %all-reduce.2.cloned.1.call-start = ((), (), s32[]{:S(2)}) async-start(), calls=%async_computation.1 | async-start | bytes 262144 | tf_op jit(solution)/shard_map/while/body/eval_jaxpr/psum | solution.py:38
  24.8 193.2 %reduce-scatter.2.cloned.1.call-start = ((), (), s32[]{:S(2)}) async-start(), calls=%async_computation.2 | async-start | bytes 2129920 | tf_op jit(solution)/shard_map/while/body/eval_jaxpr/reduce_scatter | solution.py:42
  79.3 222.5 %all-gather.2.cloned.1.call-start = ((), (), s32[]{:S(2)}) async-start(), calls=%async_computation.3 | async-start | bytes 2129920 | tf_op jit(solution)/shard_map/while/body/eval_jaxpr/all_gather | solution.py:43
  307.8 44.3 %all-reduce.2.cloned.1.call-start = ((), (), s32[]{:S(2)}) async-start(), calls=%async_computation.1 | async-start | bytes 262144 | tf_op jit(solution)/shard_map/while/body/eval_jaxpr/psum | solution.py:38
  309.6 184.9 %reduce-scatter.2.cloned.1.call-start = ((), (), s32[]{:S(2)}) async-start(), calls=%async_computation.2 | async-start | bytes 2129920 | tf_op jit(solution)/shard_map/while/body/eval_jaxpr/reduce_scatter | solution.py:42
  356.2 222.2 %all-gather.2.cloned.1.call-start = ((), (), s32[]{:S(2)}) async-start(), calls=%async_computation.3 | async-start | bytes 2129920 | tf_op jit(solution)/shard_map/while/body/eval_jaxpr/all_gather | solution.py:43
  584.4 44.6 %all-reduce.2.cloned.1.call-start = ((), (), s32[]{:S(2)}) async-start(), calls=%async_computation.1 | async-start | bytes 262144 | tf_op jit(solution)/shard_map/while/body/eval_jaxpr/psum | solution.py:38
  586.2 185.7 %reduce-scatter.2.cloned.1.call-start = ((), (), s32[]{:S(2)}) async-start(), calls=%async_computation.2 | async-start | bytes 2129920 | tf_op jit(solution)/shard_map/while/body/eval_jaxpr/reduce_scatter | solution.py:42
  633.2 222.5 %all-gather.2.cloned.1.call-start = ((), (), s32[]{:S(2)}) async-start(), calls=%async_computation.3 | async-start | bytes 2129920 | tf_op jit(solution)/shard_map/while/body/eval_jaxpr/all_gather | solution.py:43
Sparse Core Ops, SparseCore 0:
  27.2 47.9 all-reduce.1
  79.8 138.1 reduce-scatter.1
  220.8 81.0 all-gather.1
  310.7 41.4 all-reduce.1
  356.6 137.9 reduce-scatter.1
  497.1 81.3 all-gather.1
  587.6 41.4 all-reduce.1
  633.6 138.1 reduce-scatter.1
  774.6 81.0 all-gather.1
where the time goes:
time: 869 us; the launch traced here: 868 us
  waiting for transfers between devices  799 us (92%)
  matrix products  32.3 us (4%)
  local copies, waits for them, and re-layouts  19.7 us (2%)
  between operations  13.1 us (2%)
    reduce_scatter x3, waiting for transfers between devices, advance(): own_rows = lax.psum_scatter(product, 'row', scatter_dimension=0, tiled=True)  415 us
    all_gather x3, waiting for transfers between devices, advance(): quarter = lax.all_gather(own_rows, 'row', axis=0, tiled=True)  247 us
    psum x3, waiting for transfers between devices, advance(): summed = lax.psum(own_partial, 'col')  136 us
    dot_general x3, matrix products, update(): change = jnp.einsum('piq,qm->pim', column_slab, quarter, precision=highest)  17.9 us
  transfers between devices with their start and end apart: 9, of which 9 were waited for; matrix products, arithmetic and copies ran while one was open for 0% of the time, Pallas kernels for 0%

commit v1 on v0

--- a/solution.py
+++ b/solution.py
@@ -35,7 +35,9 @@
     def advance(panel, loop_state):
         partial_rows, solved, pending = loop_state
         own_partial = lax.dynamic_index_in_dim(partial_rows, panel, 0, keepdims=False)
-        summed = lax.psum(own_partial, "col")
+        summed = own_partial
+        for hop in (1, 2):
+            summed = summed + lax.ppermute(summed, "col", [(dev, dev ^ hop) for dev in range(4)])
         residual = lax.dynamic_index_in_dim(kernel, panel, 0, keepdims=False) - summed
         inverse_block = lax.dynamic_index_in_dim(inverse_blocks, panel, 0, keepdims=False)
         product = jnp.einsum("iq,im->qm", inverse_block, residual, precision=highest)

time: 869 us -> 759 us (0.87)
  waiting for transfers between devices: 799 us -> 677 us
  starting transfers between devices: 0.3 us -> 14 us
    psum x3 -> x0, waiting for transfers between devices: 136 us -> none  [advance(): summed = lax.psum(own_partial, 'col')]
    ppermute x0 -> x6, waiting for transfers between devices: none -> 17.3 us  [advance(): lax.ppermute(summed, 'col', [(dev, dev ^ hop) for dev in range(4)])]
    ppermute x0 -> x6, starting transfers between devices: none -> 13.9 us  [advance(): lax.ppermute(summed, 'col', [(dev, dev ^ hop) for dev in range(4)])]
  transfers between devices with their start and end apart: 9 -> 12, of which waited for: 9 -> 12; matrix products, arithmetic and copies ran while one was open for 0% -> 1% of each run, Pallas kernels for 0% -> 0%
where the time goes in v1:
time: 759 us; the launch traced here: 758 us
  waiting for transfers between devices  677 us (89%)
  matrix products  32.1 us (4%)
  local copies, waits for them, and re-layouts  17.7 us (2%)
  starting transfers between devices  14 us (2%)
  between operations  13.4 us (2%)
    reduce_scatter x3, waiting for transfers between devices, advance(): own_rows = lax.psum_scatter(product, 'row', scatter_dimension=0, tiled=True)  410 us
    all_gather x3, waiting for transfers between devices, advance(): quarter = lax.all_gather(own_rows, 'row', axis=0, tiled=True)  249 us
    dot_general x3, matrix products, update(): change = jnp.einsum('piq,qm->pim', column_slab, quarter, precision=highest)  17.9 us
    ppermute x6, waiting for transfers between devices, advance(): lax.ppermute(summed, 'col', [(dev, dev ^ hop) for dev in range(4)])  17.3 us
  transfers between devices with their start and end apart: 12, of which 12 were waited for; matrix products, arithmetic and copies ran while one was open for 1% of the time, Pallas kernels for 0%

profile of v1, /device:TPU:1, one launch (start us, length us, event | category | flops | bytes accessed | tf_op | source)
XLA Modules:
  0.0 758.1 jit_solution(14000335803166460265)
XLA Ops:
  6.5 0.9 fusion.28
  7.4 0.8 multiply_reduce_fusion.1
  8.3 2.0 fusion.25
  10.3 12.1 %copy.15 = f32[3,1,128,3,1,2048]{5,2,0,3,4,1:T(8,128)} copy(f32[3,1,128,3,1,2048]{5,4,3,2,1,0:T(1,128)} %param.10) | data formatting | bytes 18874368 | tf_op args[3]
  22.4 0.0 copy-done
  22.4 1.4 copy.16
  23.8 727.4 %while.16 = (s32[]{:T(128)}, f32[3,128,256]{2,1,0:T(8,128)}, f32[3,32,256]{2,1,0:T(8,128)}, f32[3,128,3,2048]{3,1,0,2:T(8,128)}, f32[3,128,2048]{2,1,0:T(8,128)S...) while((s32[]{:T(128)}, f32[3,128,256]{2,1,0:T(8,128)}, f32[3,32,256]{2,1,0:T(8,128)}, ...), condition=%wide.region_4.5_spmd.clone, body=%wide.region_2.4_spmd.clone.sunk | while | flops 3221618688 | bytes 24904992 | solution.py:55
  24.0 0.0 reduce-scatter.2.cloned.1.call-start
  24.2 2.1 collective-permute-start
  26.3 2.4 collective-permute-done
  28.7 3.6 collective-permute-start.1
  32.3 2.4 collective-permute-done.1
  34.7 4.1 fusion.40
  38.7 0.0 reduce-scatter.2.cloned.1.call-update
  38.7 0.0 all-gather.2.cloned.1.call-start
  38.8 140.9 %reduce-scatter.2.cloned.1.call-done = f32[32,256]{1,0:T(8,128)} async-done(((f32[2048,256]{1,0:T(8,128)}), f32[32,256]{1,0:T(8,128)}) %reduce-scatter.2.cloned.1.call-update) | async-done | bytes 32784 | tf_op jit(solution)/shard_map/while/body/eval_jaxpr/reduce_scatter | solution.py:44
  179.7 0.0 all-gather.2.cloned.1.call-update
  179.7 1.4 bitcast_dynamic-update-slice_fusion.2
  181.1 82.9 %all-gather.2.cloned.1.call-done = f32[2048,256]{1,0:T(8,128)} async-done(((f32[32,256]{1,0:T(8,128)}), f32[2048,256]{1,0:T(8,128)}) %all-gather.2.cloned.1.call-update) | async-done | bytes 2097168 | tf_op jit(solution)/shard_map/while/body/eval_jaxpr/all_gather | solution.py:45
  264.0 6.0 fusion.41
  270.0 0.0 reduce-scatter.2.cloned.1.call-start
  270.0 1.0 broadcast_select_fusion.2
  271.1 1.3 collective-permute-start
  272.3 3.7 collective-permute-done
  276.0 2.8 collective-permute-start.1
  278.8 2.6 collective-permute-done.1
  281.4 4.1 fusion.40
  285.5 0.0 reduce-scatter.2.cloned.1.call-update
  285.5 0.0 all-gather.2.cloned.1.call-start
  285.6 134.6 %reduce-scatter.2.cloned.1.call-done = f32[32,256]{1,0:T(8,128)} async-done(((f32[2048,256]{1,0:T(8,128)}), f32[32,256]{1,0:T(8,128)}) %reduce-scatter.2.cloned.1.call-update) | async-done | bytes 32784 | tf_op jit(solution)/shard_map/while/body/eval_jaxpr/reduce_scatter | solution.py:44
  420.1 0.0 all-gather.2.cloned.1.call-update
  420.2 1.4 bitcast_dynamic-update-slice_fusion.2
  421.6 83.1 %all-gather.2.cloned.1.call-done = f32[2048,256]{1,0:T(8,128)} async-done(((f32[32,256]{1,0:T(8,128)}), f32[2048,256]{1,0:T(8,128)}) %all-gather.2.cloned.1.call-update) | async-done | bytes 2097168 | tf_op jit(solution)/shard_map/while/body/eval_jaxpr/all_gather | solution.py:45
  504.7 6.0 fusion.41
  510.6 0.0 reduce-scatter.2.cloned.1.call-start
  510.6 1.0 broadcast_select_fusion.2
  511.7 1.3 collective-permute-start
  513.0 3.7 collective-permute-done
  516.6 2.8 collective-permute-start.1
  519.4 2.6 collective-permute-done.1
  522.1 4.1 fusion.40
  526.1 0.0 reduce-scatter.2.cloned.1.call-update
  526.1 0.0 all-gather.2.cloned.1.call-start
  526.2 134.9 %reduce-scatter.2.cloned.1.call-done = f32[32,256]{1,0:T(8,128)} async-done(((f32[2048,256]{1,0:T(8,128)}), f32[32,256]{1,0:T(8,128)}) %reduce-scatter.2.cloned.1.call-update) | async-done | bytes 32784 | tf_op jit(solution)/shard_map/while/body/eval_jaxpr/reduce_scatter | solution.py:44
  661.1 0.0 all-gather.2.cloned.1.call-update
  661.1 1.4 bitcast_dynamic-update-slice_fusion.2
  662.5 82.8 %all-gather.2.cloned.1.call-done = f32[2048,256]{1,0:T(8,128)} async-done(((f32[32,256]{1,0:T(8,128)}), f32[2048,256]{1,0:T(8,128)}) %all-gather.2.cloned.1.call-update) | async-done | bytes 2097168 | tf_op jit(solution)/shard_map/while/body/eval_jaxpr/all_gather | solution.py:45
  745.3 6.0 fusion.41
  (13 shorter events, 0.2 us)
Async XLA Ops:
  10.3 12.1 %copy-start = (f32[3,1,128,1,2048]{4,3,2,1,0:T(1,128)S(1)}, f32[3,1,128,1,2048]{4,3,2,1,0:T(1,128)}, u32[]{:S(2)}) copy-start(f32[3,1,128,1,2048]{4,3,2,1,0:T(1,128)} %param.11) | copy-start | bytes 9437188
  24.0 155.7 %reduce-scatter.2.cloned.1.call-start = ((), (), s32[]{:S(2)}) async-start(), calls=%async_computation.1 | async-start | bytes 2129920 | tf_op jit(solution)/shard_map/while/body/eval_jaxpr/reduce_scatter | solution.py:44
  24.2 4.5 collective-permute-start
  28.7 6.0 collective-permute-start.1
  38.7 225.3 %all-gather.2.cloned.1.call-start = ((), (), s32[]{:S(2)}) async-start(), calls=%async_computation.2 | async-start | bytes 2129920 | tf_op jit(solution)/shard_map/while/body/eval_jaxpr/all_gather | solution.py:45
  270.0 150.1 %reduce-scatter.2.cloned.1.call-start = ((), (), s32[]{:S(2)}) async-start(), calls=%async_computation.1 | async-start | bytes 2129920 | tf_op jit(solution)/shard_map/while/body/eval_jaxpr/reduce_scatter | solution.py:44
  271.1 4.9 collective-permute-start
  276.0 5.4 collective-permute-start.1
  285.5 219.2 %all-gather.2.cloned.1.call-start = ((), (), s32[]{:S(2)}) async-start(), calls=%async_computation.2 | async-start | bytes 2129920 | tf_op jit(solution)/shard_map/while/body/eval_jaxpr/all_gather | solution.py:45
  510.6 150.5 %reduce-scatter.2.cloned.1.call-start = ((), (), s32[]{:S(2)}) async-start(), calls=%async_computation.1 | async-start | bytes 2129920 | tf_op jit(solution)/shard_map/while/body/eval_jaxpr/reduce_scatter | solution.py:44
  511.7 4.9 collective-permute-start
  516.6 5.4 collective-permute-start.1
  526.1 219.1 %all-gather.2.cloned.1.call-start = ((), (), s32[]{:S(2)}) async-start(), calls=%async_computation.2 | async-start | bytes 2129920 | tf_op jit(solution)/shard_map/while/body/eval_jaxpr/all_gather | solution.py:45
Sparse Core Ops, SparseCore 0:
  38.9 140.7 reduce-scatter.1
  182.8 81.1 all-gather.1
  285.6 134.4 reduce-scatter.1
  423.1 81.4 all-gather.1
  526.3 134.7 reduce-scatter.1
  664.1 81.1 all-gather.1
